TPU v7x, 256 devices: a whole 4x4x8 slice. The times are simulated.
256 devices in a mesh: seg: 8 (over y, core), chan: 32 (over z, x).
Axes of the slice: x: 4, y: 4, z: 8, core: 2. Of those that a mesh axis runs over, the one named last changes fastest.
Arguments:
- spectra: bfloat16 [8, 8192, 2, 2048], P('seg', 'chan'), may hold values from -40 to 40
- source_ids: int32 [64], replicated, may hold values from 0 to 8191, as said below
- pair_source: int32 [32768], P('chan'), may hold values from 0 to 63
- pair_offset: int32 [32768], P('chan'), may hold values from -128 to 383, as said below
- pair_counts: int32 [32], P('chan'), may hold values from 256 to 1024, as said below
Outputs:
- correlations: float32 [1024, 32768], P('seg', 'chan')
Inputs may be any that keep to these rules, and one draw needn't show every extreme that they name: `source_ids`: distinct channels. `pair_offset`: blocks at the fibre's ends never reach beyond it: block 0 has offsets of 0 or more, the last block offsets under 256. `pair_counts`: one block holds exactly 1024 live slots in every draw; the others hold 256 to 768.
All inputs are finite; a program needn't handle non-finite values.
Results may differ from a plain program's by a relative error of at most 0.0055.
Values may be sent and summed in bfloat16 or wider, within the bound.
A program may use at most 192 MiB of HBM per device.

v0:
```python
import math

import jax
import jax.numpy as jnp
from jax import lax
from jax.sharding import PartitionSpec as P

LAGS = 1024
WBLOCK = 64


def extended_2(cells, sides, width):
    for axis, dim in sides:
        count = lax.axis_size(axis)
        ends = count - 1
        head = lax.slice_in_dim(cells, 0, width, axis=dim)
        tail = lax.slice_in_dim(cells, cells.shape[dim] - width, cells.shape[dim], axis=dim)
        cells = jnp.concatenate(
            [
                lax.ppermute(tail, axis, [(i, (i + 1) % count) for i in range(ends)]),
                cells,
                lax.ppermute(head, axis, [((i + 1) % count, i) for i in range(ends)]),
            ],
            axis=dim,
        )
    return cells


def whiten(values):
    power = values[..., 0, :] ** 2 + values[..., 1, :] ** 2
    grouped = power.reshape(power.shape[:-1] + (power.shape[-1] // WBLOCK, WBLOCK))
    level = jnp.mean(grouped, axis=-1)
    inverse = lax.rsqrt(level + 1e-06)
    spread = jnp.repeat(inverse, WBLOCK, axis=-1)
    return (values * spread[..., None, :]).astype(jnp.bfloat16)


def lag_matrix(count, total_segs, bin_count):
    lag_steps = jnp.arange(count, dtype=jnp.int32) - LAGS // 2
    bin_steps = jnp.arange(bin_count, dtype=jnp.int32)
    phase = jnp.mod(lag_steps[:, None] * bin_steps[None, :], 2 * bin_count).astype(jnp.float32)
    theta = phase * (math.pi / bin_count)
    factor = 1.0 / math.sqrt(bin_count * total_segs)
    return jnp.concatenate([jnp.cos(theta) * factor, -jnp.sin(theta) * factor], axis=1).astype(
        jnp.bfloat16
    )


def cross_spectrum(source_rows, receiver_rows, live_slots):
    src_f = source_rows.astype(jnp.float32)
    rec_f = receiver_rows.astype(jnp.float32)
    real_part = src_f[:, 0] * rec_f[:, 0] + src_f[:, 1] * rec_f[:, 1]
    imag_part = src_f[:, 1] * rec_f[:, 0] - src_f[:, 0] * rec_f[:, 1]
    joined = jnp.concatenate([real_part, imag_part], axis=1).astype(jnp.bfloat16)
    return jnp.where(live_slots[:, None], joined, jnp.zeros_like(joined))


def transform_live(lag_table, cross_list, live_count, tile_width):
    row_count = lag_table.shape[0]
    column_count = cross_list[0].shape[0]
    trips = (live_count + tile_width - 1) // tile_width

    def one_tile(index, accum):
        part_sum = jnp.zeros((row_count, tile_width), jnp.float32)
        for cross_spec in cross_list:
            piece = lax.dynamic_slice_in_dim(cross_spec, index * tile_width, tile_width, 0)
            part_sum = lax.dot_general(
                lag_table, piece, (((1,), (1,)), ((), ())), preferred_element_type=jnp.float32
            )
        return lax.dynamic_update_slice_in_dim(accum, part_sum, index * tile_width, 1)

    return lax.fori_loop(0, trips, one_tile, jnp.zeros((row_count, column_count), jnp.float32))


def per_device(spectra, source_ids, pair_source, pair_offset, pair_counts):
    seg_local = spectra.shape[0]
    chan_rows = spectra.shape[1]
    bin_count = spectra.shape[3]
    band_width = chan_rows // 2
    seg_devices = lax.axis_size("seg")
    total_segs = seg_local * seg_devices
    whitened = whiten(spectra.astype(jnp.float32))
    first_chan = lax.axis_index("chan") * chan_rows
    local_ids = source_ids - first_chan
    selector = (local_ids[:, None] == jnp.arange(chan_rows, dtype=jnp.int32)[None, :]).astype(
        jnp.bfloat16
    )
    picked = jnp.einsum("nc,scrf->snrf", selector, whitened, preferred_element_type=jnp.float32)
    sources = lax.psum(picked.astype(jnp.bfloat16), "chan")
    extended = extended_2(whitened, (("chan", 1),), band_width)
    pair_rows = pair_offset + band_width
    pair_total = pair_source.shape[0]
    quarter_slots = pair_total // 4
    tile_width = min(128, quarter_slots)
    own_count = pair_counts[0]
    live_slots = jnp.arange(pair_total, dtype=jnp.int32) < own_count
    crosses = [cross_spectrum(sources[0][pair_source], extended[0][pair_rows], live_slots)]
    lag_rows = LAGS // seg_devices
    lag_table = lag_matrix(lag_rows * lax.axis_size("seg"), total_segs, bin_count)
    return lax.psum_scatter(
        transform_live(lag_table, crosses, own_count, tile_width),
        "seg",
        scatter_dimension=0,
        tiled=True,
    )


def solution(mesh):
    in_specs = (P("seg", "chan", None, None), P(), P("chan"), P("chan"), P("chan"))
    out_specs = P("seg", "chan")
    return jax.shard_map(
        per_device, mesh=mesh, in_specs=in_specs, out_specs=out_specs, check_vma=False
    )
```

profile of v0, /device:TPU:1, one launch (start us, length us, event | category | flops | bytes accessed | tf_op | source)
XLA Modules:
  0.0 432.8 jit_solution(1174280209690819535)
XLA Ops:
  6.5 2.5 copy_convert_fusion
  9.4 1.9 copy.29
  11.3 1.8 reduce_sum.9
  13.3 1.9 copy.30
  15.2 3.4 multiply_convert_fusion.2
  18.6 1.5 fusion.16
  20.0 4.9 %collective-permute-start = (bf16[1,128,2,2048]{3,1,2,0:T(8,128)(2,1)}, bf16[1,128,2,2048]{3,1,2,0:T(8,128)(2,1)}, u32[]{:S(2)}, u32[]{:S(2)}) collective-permute-start(bf16[1,128,2,2048]{3,1,2,0:T(8,128)(2,1)} %get-tuple-element.46), channel_id=1, source_target_pairs={{0,1},{1,2},{2,3},{3,4},{4,5},{5,6},{6,7},{7,8},{8,9},{9,10},{10,1... | collective-permute-start | bytes 3145736 | tf_op jit(solution)/shard_map/ppermute | solution.py:20
  24.9 1.3 collective-permute-start.1
  26.2 1.3 fusion.8
  27.6 37.3 %multiply_convert_fusion.1 = (bf16[1024,2048]{1,0:T(8,128)(2,1)}, bf16[1024,2048]{1,0:T(8,128)(2,1)}) fusion(s32[1024]{0:T(1024)S(1)} %iota_add_fusion), kind=kLoop, calls=%fused_computation.15 | loop fusion | flops 39845888 | bytes 8392704 | tf_op jit(solution)/shard_map/convert
  65.7 7.8 %pad_maximum_fusion = bf16[1024,4096]{1,0:T(8,128)(2,1)} fusion(bf16[1024,2048]{1,0:T(8,128)(2,1)} %get-tuple-element.49, bf16[1024,2048]{1,0:T(8,128)(2,1)} %get-tuple-element.48), kind=kLoop, calls=%fused_computation.13 | loop fusion | flops 16777216 | bytes 16777216 | tf_op jit(solution)/shard_map/concatenate | solution.py:44
  73.5 103.6 %all-reduce.2.cloned.1.call-done = bf16[64,2,2048]{2,0,1:T(8,128)(2,1)} async-done(((bf16[64,2,2048]{2,0,1:T(8,128)(2,1)}), bf16[64,2,2048]{2,0,1:T(8,128)(2,1)}) %all-reduce.2.cloned.1.call-update) | async-done | bytes 524304 | tf_op jit(solution)/shard_map/psum | solution.py:89
  177.2 1.6 copy.31
  178.7 25.1 %gather_fusion = bf16[1024,2,2048]{2,1,0:T(2,128)(2,1)} fusion(bf16[64,2,2048]{2,1,0:T(2,128)(2,1)S(1)} %copy.31, s32[1024]{0:T(1024)S(1)} %fusion.14), kind=kCustom, calls=%fused_computation | custom fusion | bytes 16781312 | tf_op jit(solution)/shard_map/gather | solution.py:97
  203.9 11.7 %convert_element_type.34 = f32[1024,2,2048]{2,1,0:T(2,128)} convert(bf16[1024,2,2048]{2,1,0:T(2,128)(2,1)} %gather_fusion) | non-fusion elementwise | flops 4194304 | bytes 25165824 | tf_op jit(solution)/shard_map/convert_element_type | solution.py:50
  215.7 3.3 maximum_bitcast_fusion
  219.0 8.5 %copy.32 = bf16[512,2,2048]{2,1,0:T(2,128)(2,1)} copy(bf16[512,2,2048]{2,0,1:T(8,128)(2,1)} %maximum_bitcast_fusion) | data formatting | bytes 8388608 | tf_op jit(solution)/shard_map/squeeze | solution.py:97
  227.5 27.3 %gather_fusion.1 = bf16[1024,2,2048]{2,1,0:T(2,128)(2,1)} fusion(bf16[512,2,2048]{2,1,0:T(2,128)(2,1)} %copy.32, s32[1024]{0:T(1024)S(1)} %fusion.15), kind=kCustom, calls=%fused_computation.1 | custom fusion | bytes 16781312 | tf_op jit(solution)/shard_map/gather | solution.py:97
  254.8 11.8 %convert_element_type.35 = f32[1024,2,2048]{2,1,0:T(2,128)} convert(bf16[1024,2,2048]{2,1,0:T(2,128)(2,1)} %gather_fusion.1) | non-fusion elementwise | flops 4194304 | bytes 25165824 | tf_op jit(solution)/shard_map/convert_element_type | solution.py:51
  266.6 40.9 %add_convert_fusion = (bf16[1024,1,2048]{2,1,0:T(2,128)(2,1)}, bf16[1024,1,2048]{2,1,0:T(2,128)(2,1)}) fusion(f32[1024,2,2048]{2,1,0:T(2,128)} %convert_element_type.35, f32[1024,2,2048]{2,1,0:T(2,128)} %convert_element_type.34), kind=kLoop, calls=%fused_computation.19 | loop fusion | flops 16777216 | bytes 41943040 | tf_op jit(solution)/shard_map/convert.5
  307.5 12.9 %copy_bitcast_fusion = (bf16[1024,2048]{1,0:T(8,128)(2,1)S(1)}, bf16[1024,2048]{1,0:T(8,128)(2,1)S(1)}) fusion(bf16[1024,1,2048]{2,1,0:T(2,128)(2,1)} %get-tuple-element.45, bf16[1024,1,2048]{2,1,0:T(2,128)(2,1)} %get-tuple-element.44), kind=kLoop, calls=%fused_computation.22 | loop fusion | bytes 16777216
  320.4 4.6 %maximum_select_fusion = bf16[1024,4096]{1,0:T(8,128)(2,1)} fusion(bf16[1024,2048]{1,0:T(8,128)(2,1)S(1)} %get-tuple-element.50, bf16[1024,2048]{1,0:T(8,128)(2,1)S(1)} %get-tuple-element.51, pred[1024]{0:T(1024)(128)(4,1)S(1)} %iota_compare_fusion.1), kind=kLoop, calls=%fused_computation.12 | loop fusion | flops 20971520 | bytes 16778240 | tf_op jit(solution)/shard_map/jit(_where)/select_n | solution.py:55
  324.9 2.5 broadcast_in_dim.30.clone
  327.4 38.5 %while.10 = (s32[]{:T(128)}, f32[1024,1024]{1,0:T(8,128)}, s32[]{:T(128)}, bf16[1024,4096]{1,0:T(8,128)(2,1)}, bf16[1024,4096]{1,0:T(8,128)(2,1)}, /*index=5*/s32[]{:T(128)}, s32[]{:T(128)}, s32[]{:T(128)}, s32[]{:T(128)}) while((s32[]{:T(128)}, f32[1024,1024]{1,0:T(8,128)}, s32[]{:T(128)}, bf16[1024,4096]{1,0:T(8,128)(2,1)}, ...), condition=%wide.region_3.4_spmd, body=%wide.region_2.3_spmd.sunk | while | flops 1073741824 | bytes 12058771 | solution.py:72
  327.4 6.6 %convolution_bitcast_fusion.2 = f32[1024,128]{0,1:T(8,128)S(1)} fusion(bf16[1024,4096]{1,0:T(8,128)(2,1)} %get-tuple-element.106, bf16[1024,4096]{1,0:T(8,128)(2,1)} %get-tuple-element.105, s32[]{:T(128)S(6)} %select_n.49), kind=kOutput, calls=%fused_computation.2.clone.1 | convolution fusion | flops 1073741824 | bytes 9961476 | tf_op jit(solution)/shard_map/while/body/dot_general | solution.py:67
  335.1 6.6 %convolution_bitcast_fusion.2 = f32[1024,128]{0,1:T(8,128)S(1)} fusion(bf16[1024,4096]{1,0:T(8,128)(2,1)} %get-tuple-element.106, bf16[1024,4096]{1,0:T(8,128)(2,1)} %get-tuple-element.105, s32[]{:T(128)S(6)} %select_n.49), kind=kOutput, calls=%fused_computation.2.clone.1 | convolution fusion | flops 1073741824 | bytes 9961476 | tf_op jit(solution)/shard_map/while/body/dot_general | solution.py:67
  342.8 6.6 %convolution_bitcast_fusion.2 = f32[1024,128]{0,1:T(8,128)S(1)} fusion(bf16[1024,4096]{1,0:T(8,128)(2,1)} %get-tuple-element.106, bf16[1024,4096]{1,0:T(8,128)(2,1)} %get-tuple-element.105, s32[]{:T(128)S(6)} %select_n.49), kind=kOutput, calls=%fused_computation.2.clone.1 | convolution fusion | flops 1073741824 | bytes 9961476 | tf_op jit(solution)/shard_map/while/body/dot_general | solution.py:67
  349.6 0.9 constant_dynamic-update-slice_fusion.2
  350.5 6.6 %convolution_bitcast_fusion.2 = f32[1024,128]{0,1:T(8,128)S(1)} fusion(bf16[1024,4096]{1,0:T(8,128)(2,1)} %get-tuple-element.106, bf16[1024,4096]{1,0:T(8,128)(2,1)} %get-tuple-element.105, s32[]{:T(128)S(6)} %select_n.49), kind=kOutput, calls=%fused_computation.2.clone.1 | convolution fusion | flops 1073741824 | bytes 9961476 | tf_op jit(solution)/shard_map/while/body/dot_general | solution.py:67
  358.2 6.6 %convolution_bitcast_fusion.2 = f32[1024,128]{0,1:T(8,128)S(1)} fusion(bf16[1024,4096]{1,0:T(8,128)(2,1)} %get-tuple-element.106, bf16[1024,4096]{1,0:T(8,128)(2,1)} %get-tuple-element.105, s32[]{:T(128)S(6)} %select_n.49), kind=kOutput, calls=%fused_computation.2.clone.1 | convolution fusion | flops 1073741824 | bytes 9961476 | tf_op jit(solution)/shard_map/while/body/dot_general | solution.py:67
  365.0 0.9 constant_dynamic-update-slice_fusion.2
  366.0 60.0 %reduce-scatter.2.cloned.1.call-done = f32[128,1024]{1,0:T(8,128)} async-done(((f32[1024,1024]{1,0:T(8,128)}), f32[128,1024]{1,0:T(8,128)}) %reduce-scatter.2.cloned.1.call-update) | async-done | bytes 524304 | tf_op jit(solution)/shard_map/reduce_scatter | solution.py:100
  (28 shorter events, 4.2 us)
Async XLA Ops:
  6.5 170.6 %all-reduce.2.cloned.1.call-start = ((), (), s32[]{:S(2)}) async-start(), calls=%async_computation.1 | async-start | bytes 1048576 | tf_op jit(solution)/shard_map/psum | solution.py:89
  13.1 13.1 %copy-start.2 = (s32[64]{0:T(128)S(1)}, s32[64]{0:T(128)}, u32[]{:S(2)}) copy-start(s32[64]{0:T(128)} %param.8) | copy-start | bytes 772
  18.5 46.4 %copy-start = (s32[1024]{0:T(1024)S(1)}, s32[1024]{0:T(1024)}, u32[]{:S(2)}) copy-start(s32[1024]{0:T(1024)} %param.10) | copy-start | bytes 12292
  18.6 47.1 %copy-start.1 = (s32[1024]{0:T(1024)S(1)}, s32[1024]{0:T(1024)}, u32[]{:S(2)}) copy-start(s32[1024]{0:T(1024)} %param.9) | copy-start | bytes 12292
  20.0 195.6 %collective-permute-start = (bf16[1,128,2,2048]{3,1,2,0:T(8,128)(2,1)}, bf16[1,128,2,2048]{3,1,2,0:T(8,128)(2,1)}, u32[]{:S(2)}, u32[]{:S(2)}) collective-permute-start(bf16[1,128,2,2048]{3,1,2,0:T(8,128)(2,1)} %get-tuple-element.46), channel_id=1, source_target_pairs={{0,1},{1,2},{2,3},{3,4},{4,5},{5,6},{6,7},{7,8},{8,9},{9,10},{10,1... | collective-permute-start | bytes 3145736 | tf_op jit(solution)/shard_map/ppermute | solution.py:20
  24.9 190.7 %collective-permute-start.1 = (bf16[1,128,2,2048]{3,1,2,0:T(8,128)(2,1)}, bf16[1,128,2,2048]{3,1,2,0:T(8,128)(2,1)}, u32[]{:S(2)}, u32[]{:S(2)}) collective-permute-start(bf16[1,128,2,2048]{3,1,2,0:T(8,128)(2,1)} %get-tuple-element.47), channel_id=1, source_target_pairs={{1,0},{2,1},{3,2},{4,3},{5,4},{6,5},{7,6},{8,7},{9,8},{10,9},{11,1... | collective-permute-start | bytes 3145736 | tf_op jit(solution)/shard_map/ppermute | solution.py:22
  27.6 398.4 %reduce-scatter.2.cloned.1.call-start = ((), (), s32[]{:S(2)}) async-start(), calls=%async_computation.2 | async-start | bytes 4718592 | tf_op jit(solution)/shard_map/reduce_scatter | solution.py:100
Sparse Core Ops, SparseCore 0:
  27.7 149.4 all-reduce.1
  366.1 59.8 reduce-scatter.1
where the time goes:
time: 436 us; the launch traced here: 433 us
  waiting for transfers between devices  164 us (38%)
  other arithmetic  126 us (29%)
  local copies, waits for them, and re-layouts  88.7 us (20%)
  matrix products  34.4 us (8%)
  between operations  14.2 us (3%)
  starting transfers between devices  6.22 us (1%)
    psum x1, waiting for transfers between devices, per_device(): sources = lax.psum(picked.astype(jnp.bfloat16), 'chan')  104 us
    another operation x2, other arithmetic  78.2 us
    reduce_scatter x1, waiting for transfers between devices, per_device(): lax.psum_scatter(transform_live(lag_table, crosses, own_count, tile_width...  60 us
    dot_general x5, matrix products, one_tile(): lax.dot_general(lag_table, piece, (((1,), (1,)), ((), ())), preferred_ele...  33.1 us
    gather x1, local copies, waits for them, and re-layouts, per_device(): extended[0][pair_rows]  27.3 us
    gather x1, local copies, waits for them, and re-layouts, per_device(): sources[0][pair_source]  25.1 us
    unnamed x7, local copies, waits for them, and re-layouts  12.9 us
    convert_element_type x1, other arithmetic, cross_spectrum(): rec_f = receiver_rows.astype(jnp.float32)  11.8 us
  transfers between devices with their start and end apart: 4, of which 2 were waited for; matrix products, arithmetic and copies ran while one was open for 20% of the time, Pallas kernels for 0%

commit v1 on v0

v1 whole, which is shorter than its diff:
```python
import functools
import math

import jax
import jax.numpy as jnp
import ml_dtypes
import numpy as np
from jax import lax
from jax.experimental import pallas as pl
from jax.experimental.pallas import tpu as pltpu
from jax.sharding import PartitionSpec as P

MESH = pl.DeviceIdType.MESH
WBLOCK = 64
BINS = 256
TILE = 256
CORES = 2
NX = 4


def lag_table(lags, freq, segs):
    tau = np.arange(lags, dtype=np.int64)[:, None] - lags // 2
    phase = np.mod(tau * np.arange(freq, dtype=np.int64)[None, :], 2 * freq)
    theta = phase * (math.pi / freq)
    scale = 1.0 / math.sqrt(freq * segs)
    both = np.stack([np.cos(theta) * scale, -np.sin(theta) * scale])
    both = both.astype(np.float32).astype(ml_dtypes.bfloat16)
    chunks = freq // BINS
    both = both.reshape(2, lags, chunks, BINS).transpose(2, 1, 0, 3)
    return both.reshape(chunks, lags, 2 * BINS)


def dot(a, b):
    return jnp.dot(a, b, preferred_element_type=jnp.float32)


def kernel(
    nz, ny, ids_ref, psrc_ref, poff_ref, cnt_ref, raw_ref, tab_hbm, out_ref,
    tab, rows, pick, slab_in, slab, part_in, srcs, src_t, hot_r, hot_s, acc,
    core_out, core_in, y_out, y_in, y_own,
    tab_sem, halo_send, halo_recv, x1_send, x1_recv, z1_send, z1_recv,
    z2_send, z2_recv, x2_send, x2_recv, core_send, core_recv, y_send, y_recv,
):
    chunks, _, chans, _ = raw_ref.shape
    band = chans // 2
    slots = psrc_ref.shape[1]
    n_src = pick.shape[1]
    tiles = slots // TILE
    out_rows = out_ref.shape[0]
    per = pick.shape[0] // (NX * nz)
    seg, chan = lax.axis_index("seg"), lax.axis_index("chan")
    n_chan = NX * nz
    my, mc = seg // CORES, seg % CORES
    mz, mx = chan // NX, chan % NX
    left, right = (chan + n_chan - 1) % n_chan, (chan + 1) % n_chan
    other = my * CORES + (1 - mc)

    def x_peer(d):
        return mz * NX + (mx + d) % NX

    def z_peer(d):
        return ((mz + d) % nz) * NX + mx

    def y_peer(d):
        return ((my + d) % ny) * CORES + mc

    def remote(src, dst, send, recv, **where):
        return pltpu.make_async_remote_copy(
            src_ref=src, dst_ref=dst, send_sem=send, recv_sem=recv,
            device_id=where, device_id_type=MESH,
        )

    for f in range(chunks):
        pltpu.make_async_copy(tab_hbm.at[f], tab.at[f], tab_sem.at[f]).start()

    barrier = pltpu.get_barrier_semaphore()
    met = 0
    for peer in [left, right] + [x_peer(d) for d in range(1, NX)] + [z_peer(d) for d in range(1, nz)]:
        pl.semaphore_signal(barrier, inc=1, device_id={"chan": peer}, device_id_type=MESH)
        met += 1
    for peer in [other] + [y_peer(d) for d in range(1, ny)]:
        pl.semaphore_signal(barrier, inc=1, device_id={"seg": peer}, device_id_type=MESH)
        met += 1
    pl.semaphore_wait(barrier, met)

    def halo_left(f):
        return remote(
            rows.at[f, :, pl.ds(band, band)], rows.at[f, :, pl.ds(band + chans, band)],
            halo_send.at[0, f], halo_recv.at[0, f], chan=left,
        )

    def halo_right(f):
        return remote(
            rows.at[f, :, pl.ds(2 * band, band)], rows.at[f, :, pl.ds(0, band)],
            halo_send.at[1, f], halo_recv.at[1, f], chan=right,
        )

    lane = lax.broadcasted_iota(jnp.int32, (BINS, BINS), 1)
    sub = lax.broadcasted_iota(jnp.int32, (BINS, BINS), 0)
    mean_of = jnp.where(lane // WBLOCK == sub // WBLOCK, 1.0 / WBLOCK, 0.0).astype(jnp.bfloat16)
    local = ids_ref[...] - chan * chans
    sel_t = jnp.where(
        lax.broadcasted_iota(jnp.int32, (chans, local.shape[1]), 0) == local, 1.0, 0.0
    )
    sel = jnp.transpose(sel_t)[:n_src].astype(jnp.bfloat16)

    def whiten(f, carry):
        re = raw_ref[f, 0].astype(jnp.float32)
        im = raw_ref[f, 1].astype(jnp.float32)
        power = re * re + im * im
        hi = power.astype(jnp.bfloat16)
        rest = power - hi.astype(jnp.float32)
        mid = rest.astype(jnp.bfloat16)
        low = (rest - mid.astype(jnp.float32)).astype(jnp.bfloat16)
        level = dot(hi, mean_of) + (dot(mid, mean_of) + dot(low, mean_of))
        inverse = lax.rsqrt(level + 1e-06)
        for p, val in enumerate((re, im)):
            white = (val * inverse).astype(jnp.bfloat16)
            got = dot(sel, white).astype(jnp.bfloat16)
            for h in range(2):
                pick[f * 4 + p * 2 + h] = got[:, h * 128:(h + 1) * 128]
            rows[f, pl.ds(p * BINS, BINS), pl.ds(band, chans)] = jnp.transpose(white)
        halo_left(f).start()
        halo_right(f).start()
        return carry

    lax.fori_loop(0, chunks, whiten, 0)

    step = per * nz

    def x1(d):
        return remote(
            pick.at[pl.ds(((mx + d) % NX) * step, step)], slab_in.at[d - 1],
            x1_send.at[d - 1], x1_recv.at[d - 1], chan=x_peer(d),
        )

    def z1(d):
        return remote(
            slab.at[pl.ds(((mz + d) % nz) * per, per)], part_in.at[d - 1],
            z1_send.at[d - 1], z1_recv.at[d - 1], chan=z_peer(d),
        )

    mine = mx * step + mz * per

    def z2(d):
        return remote(
            srcs.at[pl.ds(mine, per)], srcs.at[pl.ds(mine, per)],
            z2_send.at[d - 1], z2_recv.at[d - 1], chan=z_peer(d),
        )

    def x2(d):
        return remote(
            srcs.at[pl.ds(mx * step, step)], srcs.at[pl.ds(mx * step, step)],
            x2_send.at[d - 1], x2_recv.at[d - 1], chan=x_peer(d),
        )

    for d in range(1, NX):
        x1(d).start()

    at = poff_ref[...] + band
    src_at = psrc_ref[...]
    live = lax.broadcasted_iota(jnp.int32, (1, slots), 1) < cnt_ref[...]
    src_at = jnp.where(live, src_at, -1)
    for t in range(tiles):
        cut = slice(t * TILE, (t + 1) * TILE)
        hot_r[t] = jnp.where(
            lax.broadcasted_iota(jnp.int32, (2 * chans, TILE), 0) == at[:, cut], 1.0, 0.0
        ).astype(jnp.bfloat16)
        hot_s[t] = jnp.where(
            lax.broadcasted_iota(jnp.int32, (n_src, TILE), 0) == src_at[:, cut], 1.0, 0.0
        ).astype(jnp.bfloat16)

    for d in range(1, NX):
        x1(d).wait_recv()
    total = pick[pl.ds(mx * step, step)]
    for d in range(1, NX):
        total = total + slab_in[d - 1]
    slab[...] = total
    for d in range(1, nz):
        z1(d).start()
    for d in range(1, nz):
        z1(d).wait_recv()
    total = slab[pl.ds(mz * per, per)]
    for d in range(1, nz):
        total = total + part_in[d - 1]
    srcs[pl.ds(mine, per)] = total
    for d in range(1, nz):
        z2(d).start()
    for d in range(1, nz):
        z2(d).wait_recv()
    for d in range(1, NX):
        x2(d).start()
    for d in range(1, NX):
        x2(d).wait_recv()

    def turn(f, carry):
        for p in range(2):
            both = jnp.concatenate([srcs[f * 4 + p * 2], srcs[f * 4 + p * 2 + 1]], axis=1)
            src_t[f, pl.ds(p * BINS, BINS), :] = jnp.transpose(both)
        return carry

    lax.fori_loop(0, chunks, turn, 0)

    def piece(f, t):
        rec = dot(rows[f], hot_r[t])
        src = dot(src_t[f], hot_s[t])
        rr, ri, sr, si = rec[:BINS], rec[BINS:], src[:BINS], src[BINS:]
        cross = jnp.concatenate([sr * rr + si * ri, si * rr - sr * ri], axis=0)
        return dot(tab[f], cross.astype(jnp.bfloat16))

    def chunk_step(f, carry):
        pltpu.make_async_copy(tab_hbm.at[f], tab.at[f], tab_sem.at[f]).wait()
        halo_left(f).wait_recv()
        halo_right(f).wait_recv()

        def first(t, c):
            acc[t] = piece(f, t)
            return c

        def more(t, c):
            acc[t] = acc[t] + piece(f, t)
            return c

        if isinstance(f, int):
            lax.fori_loop(0, tiles, first, 0)
        else:
            lax.fori_loop(0, tiles, more, 0)
        return carry

    chunk_step(0, 0)
    lax.fori_loop(1, chunks, chunk_step, 0)

    def to_core(t):
        return remote(core_out.at[t], core_in.at[t], core_send.at[t], core_recv.at[t], seg=other)

    def to_y(t, d):
        return remote(
            y_out.at[t, d - 1], y_in.at[t, d - 1],
            y_send.at[t, d - 1], y_recv.at[t, d - 1], seg=y_peer(d),
        )

    for t in range(tiles):
        for j in range(ny):
            base = (j * CORES + (1 - mc)) * out_rows
            core_out[t, j] = acc[t, pl.ds(base, out_rows)].astype(jnp.bfloat16)
        to_core(t).start()
    for t in range(tiles):
        to_core(t).wait_recv()
        for d in list(range(1, ny)) + [0]:
            j = (my + d) % ny
            base = (j * CORES + mc) * out_rows
            val = acc[t, pl.ds(base, out_rows)] + core_in[t, j].astype(jnp.float32)
            if d:
                y_out[t, d - 1] = val.astype(jnp.bfloat16)
                to_y(t, d).start()
            else:
                y_own[t] = val
    for t in range(tiles):
        val = y_own[t]
        for d in range(1, ny):
            to_y(t, d).wait_recv()
            val = val + y_in[t, d - 1].astype(jnp.float32)
        out_ref[:, t * TILE:(t + 1) * TILE] = val

    for f in range(chunks):
        halo_left(f).wait_send()
        halo_right(f).wait_send()
    for d in range(1, NX):
        x1(d).wait_send()
        x2(d).wait_send()
    for d in range(1, nz):
        z1(d).wait_send()
        z2(d).wait_send()
    for t in range(tiles):
        to_core(t).wait_send()
        for d in range(1, ny):
            to_y(t, d).wait_send()


def solution(mesh):
    ny = mesh.shape["seg"] // CORES
    nz = mesh.shape["chan"] // NX

    def per_device(table, spectra, source_ids, pair_source, pair_offset, pair_counts):
        _, chans, _, freq = spectra.shape
        chunks = freq // BINS
        slots, n_src = pair_source.shape[0], source_ids.shape[0]
        lags = table.shape[1]
        out_rows = lags // (ny * CORES)
        tiles = slots // TILE
        pieces = chunks * 4
        step = pieces // NX
        raw = spectra.reshape(chans, 2, chunks, BINS).transpose(2, 1, 0, 3)
        ids = jnp.pad(source_ids, (0, 128 - n_src), constant_values=-1).reshape(1, 128)
        bf16, f32, dma = jnp.bfloat16, jnp.float32, pltpu.SemaphoreType.DMA
        vmem = pl.BlockSpec(memory_space=pltpu.VMEM)
        return pl.pallas_call(
            functools.partial(kernel, nz, ny),
            out_shape=jax.ShapeDtypeStruct((out_rows, slots), f32),
            in_specs=[vmem] * 5 + [pl.BlockSpec(memory_space=pl.ANY)],
            out_specs=vmem,
            scratch_shapes=[
                pltpu.VMEM((chunks, lags, 2 * BINS), bf16),
                pltpu.VMEM((chunks, 2 * BINS, 2 * chans), bf16),
                pltpu.VMEM((pieces, n_src, 128), bf16),
                pltpu.VMEM((NX - 1, step, n_src, 128), bf16),
                pltpu.VMEM((step, n_src, 128), bf16),
                pltpu.VMEM((nz - 1, step // nz, n_src, 128), bf16),
                pltpu.VMEM((pieces, n_src, 128), bf16),
                pltpu.VMEM((chunks, 2 * BINS, n_src), bf16),
                pltpu.VMEM((tiles, 2 * chans, TILE), bf16),
                pltpu.VMEM((tiles, n_src, TILE), bf16),
                pltpu.VMEM((tiles, lags, TILE), f32),
                pltpu.VMEM((tiles, ny, out_rows, TILE), bf16),
                pltpu.VMEM((tiles, ny, out_rows, TILE), bf16),
                pltpu.VMEM((tiles, ny - 1, out_rows, TILE), bf16),
                pltpu.VMEM((tiles, ny - 1, out_rows, TILE), bf16),
                pltpu.VMEM((tiles, out_rows, TILE), f32),
                dma((chunks,)),
                dma((2, chunks)), dma((2, chunks)),
                dma((NX - 1,)), dma((NX - 1,)),
                dma((nz - 1,)), dma((nz - 1,)),
                dma((nz - 1,)), dma((nz - 1,)),
                dma((NX - 1,)), dma((NX - 1,)),
                dma((tiles,)), dma((tiles,)),
                dma((tiles, ny - 1)), dma((tiles, ny - 1)),
            ],
            compiler_params=pltpu.CompilerParams(
                collective_id=0, has_side_effects=True, vmem_limit_bytes=60 << 20
            ),
            name="correlate",
        )(
            ids, pair_source.reshape(1, slots), pair_offset.reshape(1, slots),
            jnp.broadcast_to(pair_counts.reshape(1, 1), (1, slots)), raw, table,
        )

    def call(spectra, source_ids, pair_source, pair_offset, pair_counts):
        freq = spectra.shape[3]
        table = jnp.asarray(lag_table(LAGS, freq, spectra.shape[0]))
        return jax.shard_map(
            per_device, mesh=mesh,
            in_specs=(P(), P("seg", "chan", None, None), P(), P("chan"), P("chan"), P("chan")),
            out_specs=P("seg", "chan"), check_vma=False,
        )(table, spectra, source_ids, pair_source, pair_offset, pair_counts)

    return call


LAGS = 1024
```

time: 436 us -> 119 us (0.27)
  waiting for transfers between devices: 164 us -> 0 us
  other arithmetic: 126 us -> 0 us
  Pallas kernels: 0 us -> 107 us
  local copies, waits for them, and re-layouts: 88.7 us -> 10.1 us
  matrix products: 34.4 us -> 0 us
  between operations: 14.2 us -> 0.68 us
  starting transfers between devices: 6.22 us -> 0 us
    pallas_call x0 -> x1, Pallas kernels: none -> 107 us  [per_device(): pl.pallas_call(functools.partial(kernel, nz, ny), out_shape=jax.ShapeDtyp...]
    psum x1 -> x0, waiting for transfers between devices: 104 us -> none  [per_device(): sources = lax.psum(picked.astype(jnp.bfloat16), 'chan')]
    another operation x2 -> x0, other arithmetic: 78.2 us -> none
    reduce_scatter x1 -> x0, waiting for transfers between devices: 60 us -> none  [per_device(): lax.psum_scatter(transform_live(lag_table, crosses, own_count, tile_width...]
    gather x2 -> x0, local copies, waits for them, and re-layouts: 52.5 us -> none  [the longest x1 27.3 us: per_device(): extended[0][pair_rows]]
    dot_general x6 -> x0, matrix products: 34.4 us -> none  [the longest x5 33.1 us: one_tile(): lax.dot_general(lag_table, piece, (((1,), (1,)), ((), ())), preferred_ele...]
    convert_element_type x4 -> x0, other arithmetic: 29.4 us -> none  [the longest x1 11.8 us: cross_spectrum(): rec_f = receiver_rows.astype(jnp.float32)]
    squeeze x1 -> x0, local copies, waits for them, and re-layouts: 8.48 us -> none  [per_device(): extended[0][pair_rows]]
  transfers between devices with their start and end apart: 4 -> 0, of which waited for: 2 -> 0; matrix products, arithmetic and copies ran while one was open for 20% -> 0% of each run, Pallas kernels for 0% -> 0%
where the time goes in v1:
time: 119 us; the launch traced here: 118 us
  Pallas kernels  107 us (90%)
  local copies, waits for them, and re-layouts  10.1 us (8%)
    pallas_call x1, Pallas kernels, per_device(): pl.pallas_call(functools.partial(kernel, nz, ny), out_shape=jax.ShapeDtyp...  107 us
    unnamed x4, local copies, waits for them, and re-layouts  6.56 us
    reshape x1, local copies, waits for them, and re-layouts, per_device(): raw = spectra.reshape(chans, 2, chunks, BINS).transpose(2, 1, 0, 3)  2.4 us

profile of v1, /device:TPU:1, one launch (start us, length us, event | category | flops | bytes accessed | tf_op | source)
XLA Modules:
  0.0 118.3 jit_solution(1134317451870273320)
XLA Ops:
  0.0 4.7 %copy.7 = bf16[1,256,2,2048]{1,3,2,0:T(8,128)(2,1)S(1)} copy(bf16[1,256,2,2048]{3,2,1,0:T(2,128)(2,1)} %param.6) | data formatting | bytes 4194304 | tf_op args[0]
  4.7 0.0 copy-start
  4.7 2.4 %copy.8 = bf16[256,2,8,256]{3,0,1,2:T(8,128)(2,1)} copy(bf16[256,2,8,256]{0,3,2,1:T(8,128)(2,1)S(1)} %bitcast.8) | data formatting | bytes 4194304 | tf_op jit(solution)/shard_map/reshape | solution.py:293
  7.7 0.6 broadcast_in_dim.8.cnt_ref
  8.3 0.0 copy-done
  8.3 0.6 pad_bitcast_fusion.ids_ref
  8.9 107.5 %correlate.1 = f32[128,1024]{1,0:T(8,128)} custom-call(s32[1,128]{1,0:T(1,128)} %pad_bitcast_fusion.ids_ref, s32[1,1024]{1,0:T(1,128)} %bitcast.10, s32[1,1024]{1,0:T(1,128)} %bitcast.11, s32[1,1024]{1,0:T(1,128)} %broadcast_in_dim.8.cnt_ref, bf16[8,2,256,256]{3,2,1,0:T(8,128)(2,1)} %bitcast.9, bf16[8,1024,512]{2,1,0:T(8,128)(2,1)} %constant.4.clone.tab_hbm), custom_call_target="tpu_custom_call" | custom-call | tf_op jit(solution)/shard_map/correlate/pallas_call | solution.py:297
  116.4 1.9 %copy.11 = f32[128,1024]{1,0:T(8,128)} copy(f32[128,1024]{1,0:T(8,128)} %correlate.1) | data formatting | bytes 1048576
Async XLA Ops:
  4.7 3.7 %copy-start = (s32[64]{0:T(128)S(1)}, s32[64]{0:T(128)}, u32[]{:S(2)}) copy-start(s32[64]{0:T(128)} %param.7) | copy-start | bytes 772

commit v2 on v1

v2 whole, which is shorter than its diff:
```python
import functools
import math

import jax
import jax.numpy as jnp
import numpy as np
from jax import lax
from jax.experimental import pallas as pl
from jax.experimental.pallas import tpu as pltpu
from jax.sharding import PartitionSpec as P

MESH = pl.DeviceIdType.MESH
LAGS = 1024
WBLOCK = 64
BINS = 256
TILE = 256
CORES = 2
NX = 4
FINE = 16
PAIRS = 2
PRE = 4
SKIP = frozenset()
PACE = (1, 2, 2)


def trig_parts(lags, freq, segs):
    scale = 1.0 / math.sqrt(freq * segs)
    coarse = lags // 2 // FINE + 1
    bins = np.arange(freq, dtype=np.int64)[None, :]

    def both(tau, factor):
        theta = np.mod(tau[:, None] * bins, 2 * freq) * (math.pi / freq)
        return np.stack([np.cos(theta) * factor, np.sin(theta) * factor]).astype(np.float32)

    return both(np.arange(coarse) * FINE, scale), both(np.arange(FINE), 1.0)


def dot(a, b):
    return jnp.dot(a, b, preferred_element_type=jnp.float32)


def kernel(
    nz, ny, ids_ref, psrc_ref, poff_ref, cnt_ref, raw_hbm, coarse_ref, fine_ref, out_ref,
    raw, tab, rows, pick, slab_in, slab, part_in, srcs, hot_r, hot_s, rec, acc,
    core_out, core_in, y_out, y_in, y_own,
    raw_sem, halo_send, halo_recv, x1_send, x1_recv, z1_send, z1_recv,
    z2_send, z2_recv, x2_send, x2_recv, core_send, core_recv, y_send, y_recv,
):
    chans = raw.shape[0]
    chunks = rows.shape[0]
    band = chans // 2
    slots = psrc_ref.shape[1]
    n_src = ids_ref.shape[1]
    tiles = slots // TILE
    out_rows = out_ref.shape[0]
    half = out_rows * ny
    part_rows = pick.shape[2]
    rounds = chunks // NX
    pairs = chunks // PAIRS
    pre = min(PRE, chunks - PAIRS)
    seg, chan = lax.axis_index("seg"), lax.axis_index("chan")
    n_chan = NX * nz
    my, mc = seg // CORES, seg % CORES
    mz, mx = chan // NX, chan % NX
    left, right = (chan + n_chan - 1) % n_chan, (chan + 1) % n_chan
    other = my * CORES + (1 - mc)

    def x_peer(d):
        return mz * NX + (mx + d) % NX

    def z_peer(d):
        return ((mz + d) % nz) * NX + mx

    def y_peer(d):
        return ((my + d) % ny) * CORES + mc

    def remote(src, dst, send, recv, **where):
        return pltpu.make_async_remote_copy(
            src_ref=src, dst_ref=dst, send_sem=send, recv_sem=recv,
            device_id=where, device_id_type=MESH,
        )

    def read(f):
        cut = pl.ds(pl.multiple_of(f * BINS, BINS), BINS)
        return pltpu.make_async_copy(raw_hbm.at[:, :, cut], raw.at[:, :, cut], raw_sem.at[f])

    for f in range(chunks):
        read(f).start()

    barrier = pltpu.get_barrier_semaphore()
    met = 0
    for peer in [left, right] + [x_peer(d) for d in range(1, NX)] + [z_peer(d) for d in range(1, nz)]:
        pl.semaphore_signal(barrier, inc=1, device_id={"chan": peer}, device_id_type=MESH)
        met += 1
    for peer in [other] + [y_peer(d) for d in range(1, ny)]:
        pl.semaphore_signal(barrier, inc=1, device_id={"seg": peer}, device_id_type=MESH)
        met += 1

    def halo_left(f):
        return remote(
            rows.at[f, :, pl.ds(band, band)], rows.at[f, :, pl.ds(band + chans, band)],
            halo_send.at[0, f], halo_recv.at[0, f], chan=left,
        )

    def halo_right(f):
        return remote(
            rows.at[f, :, pl.ds(2 * band, band)], rows.at[f, :, pl.ds(0, band)],
            halo_send.at[1, f], halo_recv.at[1, f], chan=right,
        )

    local = ids_ref[...] - chan * chans
    inside = (local >= 0) & (local < chans)
    local = jnp.concatenate(
        [jnp.where(inside, local, -1), jnp.where(inside, local + chans, -1)], axis=1
    )
    chosen = jnp.where(
        lax.broadcasted_iota(jnp.int32, (2 * chans, 2 * n_src), 0) == local, 1.0, 0.0
    ).astype(jnp.bfloat16)

    def whiten(f, carry):
        read(f).wait()
        cut = pl.ds(pl.multiple_of(f * BINS, BINS), BINS)
        re, im = [jnp.transpose(raw[:, p, cut].astype(jnp.float32)) for p in range(2)]
        power = re * re + im * im
        level = jnp.mean(power.reshape(BINS // WBLOCK, WBLOCK, chans), axis=1, keepdims=True)
        inverse = jnp.broadcast_to(
            lax.rsqrt(level + 1e-06), (BINS // WBLOCK, WBLOCK, chans)
        ).reshape(BINS, chans)
        white = [(val * inverse).astype(jnp.bfloat16) for val in (re, im)]
        for p in range(2):
            rows[f, pl.ds(p * BINS, BINS), pl.ds(band, chans)] = white[p]
        got = dot(jnp.concatenate(white, axis=1), chosen).astype(jnp.bfloat16)
        for b in range(nz):
            pick[f, b] = got[b * part_rows:(b + 1) * part_rows]
        return carry

    def x1(r, d):
        return remote(
            pick.at[r * NX + (mx + d) % NX], slab_in.at[r, d - 1],
            x1_send.at[r, d - 1], x1_recv.at[r, d - 1], chan=x_peer(d),
        )

    def z1(r, d):
        return remote(
            slab.at[r, (mz + d) % nz], part_in.at[r, d - 1],
            z1_send.at[r, d - 1], z1_recv.at[r, d - 1], chan=z_peer(d),
        )

    def z2(r, d):
        return remote(
            srcs.at[r * NX + mx, mz], srcs.at[r * NX + mx, mz],
            z2_send.at[r, d - 1], z2_recv.at[r, d - 1], chan=z_peer(d),
        )

    def x2(r, d):
        return remote(
            srcs.at[r * NX + mx], srcs.at[r * NX + mx],
            x2_send.at[r, d - 1], x2_recv.at[r, d - 1], chan=x_peer(d),
        )

    lax.fori_loop(0, chunks, whiten, 0)
    pl.semaphore_wait(barrier, met)
    for r in range(rounds):
        for d in range(1, NX):
            x1(r, d).start()

    def send_halo(f, carry):
        halo_left(f).start()
        halo_right(f).start()
        return carry

    paces = [min(sum(PACE[:i]), chunks) for i in range(len(PACE) + 1)] + [chunks]

    def send_some(stage):
        if "halo" not in SKIP:
            lax.fori_loop(paces[stage], paces[stage + 1], send_halo, 0)

    send_some(0)

    def hots():
        at = poff_ref[...] + band
        live = lax.broadcasted_iota(jnp.int32, (1, slots), 1) < cnt_ref[...]
        src_at = jnp.where(live, psrc_ref[...], -4 * n_src)
        for t in range(tiles):
            cut = slice(t * TILE, (t + 1) * TILE)
            hot_r[t] = jnp.where(
                lax.broadcasted_iota(jnp.int32, (2 * chans, TILE), 0) == at[:, cut], 1.0, 0.0
            ).astype(jnp.bfloat16)
            for p in range(2):
                hot_s[t, p] = jnp.where(
                    lax.broadcasted_iota(jnp.int32, (2 * n_src, TILE), 0)
                    == src_at[:, cut] + p * n_src, 1.0, 0.0
                ).astype(jnp.bfloat16)

    def table(i, carry):
        at = pl.ds(pl.multiple_of(i * FINE, FINE), FINE)
        for f in range(chunks):
            cut = pl.ds(f * BINS, BINS)
            c1, s1 = coarse_ref[0, pl.ds(i, 1), cut], coarse_ref[1, pl.ds(i, 1), cut]
            c2, s2 = fine_ref[0, :, cut], fine_ref[1, :, cut]
            place = pl.ds(f % PAIRS * BINS, BINS)
            tab[f // PAIRS, 0, at, place] = (c1 * c2 - s1 * s2).astype(jnp.bfloat16)
            tab[f // PAIRS, 1, at, place] = (s1 * c2 + c1 * s2).astype(jnp.bfloat16)
        return carry

    def gather(f):
        wait_halo(f)
        for t in range(tiles):
            rec[t, f] = dot(rows[f], hot_r[t]).astype(jnp.bfloat16)

    def gather_step(f, carry):
        gather(f)
        return carry

    def wait_halo(f):
        halo_left(f).wait_recv()
        halo_right(f).wait_recv()

    hots()
    lax.fori_loop(0, coarse_ref.shape[1], table, 0)
    acc[...] = jnp.zeros_like(acc)
    for r in range(rounds):
        for d in range(1, NX):
            x1(r, d).wait_recv()
        total = pick[r * NX + mx]
        for d in range(1, NX):
            total = total + slab_in[r, d - 1]
        slab[r] = total
        for d in range(1, nz):
            z1(r, d).start()
    send_some(1)
    for r in range(rounds):
        for d in range(1, nz):
            z1(r, d).wait_recv()
        total = slab[r, mz]
        for d in range(1, nz):
            total = total + part_in[r, d - 1]
        srcs[r * NX + mx, mz] = total
        for d in range(1, nz):
            z2(r, d).start()
    send_some(2)
    for r in range(rounds):
        for d in range(1, nz):
            z2(r, d).wait_recv()
        for d in range(1, NX):
            x2(r, d).start()
    send_some(3)
    lax.fori_loop(0, pre, gather_step, 0)

    def cross(f, t, early):
        got = rec[t, f].astype(jnp.float32) if early else dot(rows[f], hot_r[t])
        lhs = srcs[f].reshape(BINS, 2 * n_src)
        sr, si = dot(lhs, hot_s[t, 0]), dot(lhs, hot_s[t, 1])
        rr, ri = got[:BINS], got[BINS:]
        real, imag = sr * rr + si * ri, si * rr - sr * ri
        return real.astype(jnp.bfloat16), imag.astype(jnp.bfloat16)

    def wait_sources(r):
        for d in range(1, NX):
            x2(r, d).wait_recv()

    def pair_sum(i, t, early):
        vals = [cross(i * PAIRS + k, t, early) for k in range(PAIRS)]
        return [
            acc[t, p] + dot(tab[i, p], jnp.concatenate([v[p] for v in vals], axis=0))
            for p in range(2)
        ]

    def pair_step(early):
        def run(i, carry):
            if not early:
                for k in range(PAIRS):
                    wait_halo(i * PAIRS + k)
            for t in range(tiles):
                acc[t, 0], acc[t, 1] = pair_sum(i, t, early)
            return carry
        return run

    for r in range(rounds):
        if r * NX // PAIRS < pairs - 1:
            wait_sources(r)
        for early in (True, False):
            low, high = r * NX // PAIRS, min((r + 1) * NX // PAIRS, pairs - 1)
            if early:
                high = min(high, pre // PAIRS)
            else:
                low = max(low, pre // PAIRS)
            if low < high:
                lax.fori_loop(low, high, pair_step(early), 0)
    if (rounds - 1) * NX // PAIRS >= pairs - 1:
        wait_sources(rounds - 1)
    for k in range(PAIRS):
        wait_halo((pairs - 1) * PAIRS + k)

    def to_core(t):
        return remote(core_out.at[t], core_in.at[t], core_send.at[t], core_recv.at[t], seg=other)

    def to_y(t, d):
        return remote(
            y_out.at[t, d - 1], y_in.at[t, d - 1],
            y_send.at[t, d - 1], y_recv.at[t, d - 1], seg=y_peer(d),
        )

    def lag_block(t, j, parity):
        block = j * CORES + parity
        if j >= ny // 2:
            at = pl.ds(pl.multiple_of(block * out_rows - half, out_rows), out_rows)
            return acc[t, 0, at] - acc[t, 1, at]
        at = pl.ds(pl.multiple_of(half - (block + 1) * out_rows, out_rows), out_rows + 8)
        return (acc[t, 0, at] + acc[t, 1, at])[1:out_rows + 1]

    def finish_tile(t):
        acc[t, 0], acc[t, 1] = pair_sum(pairs - 1, t, False)
        if "rs" in SKIP:
            return
        for j in range(ny):
            core_out[t, j] = lag_block(t, j, 1 - mc).astype(jnp.bfloat16)
        to_core(t).start()

    def pass_on(t):
        to_core(t).wait_recv()
        for j in range(ny):
            y_own[t, j] = lag_block(t, j, mc) + core_in[t, j].astype(jnp.float32)
        for d in range(1, ny):
            y_out[t, d - 1] = y_own[t, (my + d) % ny].astype(jnp.bfloat16)
            to_y(t, d).start()

    for t in range(tiles):
        finish_tile(t)
        if t and "rs" not in SKIP:
            pass_on(t - 1)
    if "rs" not in SKIP:
        pass_on(tiles - 1)

    place = lax.broadcasted_iota(jnp.int32, (out_rows, out_rows), 0)
    place = jnp.where(my >= ny // 2, place, out_rows - 1 - place)
    order = jnp.where(
        lax.broadcasted_iota(jnp.int32, (out_rows, out_rows), 1) == place, 1.0, 0.0
    ).astype(jnp.bfloat16)
    for t in range(tiles):
        val = y_own[t, my]
        if "rs" not in SKIP:
            for d in range(1, ny):
                to_y(t, d).wait_recv()
                val = val + y_in[t, d - 1].astype(jnp.float32)
        high = val.astype(jnp.bfloat16)
        rest = val - high.astype(jnp.float32)
        mid = rest.astype(jnp.bfloat16)
        low = (rest - mid.astype(jnp.float32)).astype(jnp.bfloat16)
        out_ref[:, t * TILE:(t + 1) * TILE] = dot(order, high) + (dot(order, mid) + dot(order, low))

    def halo_sent(f, carry):
        halo_left(f).wait_send()
        halo_right(f).wait_send()
        return carry

    if "halo" not in SKIP:
        lax.fori_loop(0, chunks, halo_sent, 0)
    for r in range(rounds):
        for d in range(1, NX):
            x1(r, d).wait_send()
            x2(r, d).wait_send()
        for d in range(1, nz):
            z1(r, d).wait_send()
            z2(r, d).wait_send()
    if "rs" not in SKIP:
        for t in range(tiles):
            to_core(t).wait_send()
            for d in range(1, ny):
                to_y(t, d).wait_send()


def solution(mesh):
    ny = mesh.shape["seg"] // CORES
    nz = mesh.shape["chan"] // NX

    def per_device(coarse, fine, spectra, source_ids, pair_source, pair_offset, pair_counts):
        _, chans, _, freq = spectra.shape
        chunks = freq // BINS
        slots, n_src = pair_source.shape[0], source_ids.shape[0]
        out_rows = LAGS // (ny * CORES)
        tiles = slots // TILE
        rounds = chunks // NX
        part = (BINS // nz, 2 * n_src)
        taus = coarse.shape[1] * FINE
        bf16, f32, dma = jnp.bfloat16, jnp.float32, pltpu.SemaphoreType.DMA
        vmem = pl.BlockSpec(memory_space=pltpu.VMEM)
        return pl.pallas_call(
            functools.partial(kernel, nz, ny),
            out_shape=jax.ShapeDtypeStruct((out_rows, slots), f32),
            in_specs=[vmem] * 4 + [pl.BlockSpec(memory_space=pl.ANY)] + [vmem] * 2,
            out_specs=vmem,
            scratch_shapes=[
                pltpu.VMEM((chans, 2, freq), bf16),
                pltpu.VMEM((chunks // PAIRS, 2, taus, PAIRS * BINS), bf16),
                pltpu.VMEM((chunks, 2 * BINS, 2 * chans), bf16),
                pltpu.VMEM((chunks, nz, *part), bf16),
                pltpu.VMEM((rounds, NX - 1, nz, *part), bf16),
                pltpu.VMEM((rounds, nz, *part), bf16),
                pltpu.VMEM((rounds, nz - 1, *part), bf16),
                pltpu.VMEM((chunks, nz, *part), bf16),
                pltpu.VMEM((tiles, 2 * chans, TILE), bf16),
                pltpu.VMEM((tiles, 2, 2 * n_src, TILE), bf16),
                pltpu.VMEM((tiles, PRE, 2 * BINS, TILE), bf16),
                pltpu.VMEM((tiles, 2, taus, TILE), f32),
                pltpu.VMEM((tiles, ny, out_rows, TILE), bf16),
                pltpu.VMEM((tiles, ny, out_rows, TILE), bf16),
                pltpu.VMEM((tiles, ny - 1, out_rows, TILE), bf16),
                pltpu.VMEM((tiles, ny - 1, out_rows, TILE), bf16),
                pltpu.VMEM((tiles, ny, out_rows, TILE), f32),
                dma((chunks,)),
                dma((2, chunks)), dma((2, chunks)),
                dma((rounds, NX - 1)), dma((rounds, NX - 1)),
                dma((rounds, nz - 1)), dma((rounds, nz - 1)),
                dma((rounds, nz - 1)), dma((rounds, nz - 1)),
                dma((rounds, NX - 1)), dma((rounds, NX - 1)),
                dma((tiles,)), dma((tiles,)),
                dma((tiles, ny - 1)), dma((tiles, ny - 1)),
            ],
            compiler_params=pltpu.CompilerParams(
                collective_id=0, has_side_effects=True, vmem_limit_bytes=58 << 20
            ),
            name="correlate",
        )(
            source_ids.reshape(1, n_src), pair_source.reshape(1, slots),
            pair_offset.reshape(1, slots), pair_counts.reshape(1, 1), spectra[0], coarse, fine,
        )

    def call(spectra, source_ids, pair_source, pair_offset, pair_counts):
        coarse, fine = trig_parts(LAGS, spectra.shape[3], spectra.shape[0])
        return jax.shard_map(
            per_device, mesh=mesh,
            in_specs=(
                P(), P(), P("seg", "chan", None, None), P(), P("chan"), P("chan"), P("chan")
            ),
            out_specs=P("seg", "chan"), check_vma=False,
        )(
            jnp.asarray(coarse), jnp.asarray(fine),
            spectra, source_ids, pair_source, pair_offset, pair_counts,
        )

    return call
```

time: 119 us -> 83.2 us (0.70)
  Pallas kernels: 107 us -> 80.4 us
  local copies, waits for them, and re-layouts: 10.1 us -> 1.89 us
    pallas_call x1, Pallas kernels: 107 us -> 80.4 us  [per_device(): pl.pallas_call(functools.partial(kernel, nz, ny), out_shape=jax.ShapeDtyp...]
    unnamed x4 -> x1, local copies, waits for them, and re-layouts: 6.56 us -> 1.89 us
    reshape x2 -> x0, local copies, waits for them, and re-layouts: 2.98 us -> none  [the longest x1 2.4 us: per_device(): raw = spectra.reshape(chans, 2, chunks, BINS).transpose(2, 1, 0, 3)]
where the time goes in v2:
time: 83.2 us; the launch traced here: 83 us
  Pallas kernels  80.4 us (97%)
  local copies, waits for them, and re-layouts  1.89 us (2%)
    pallas_call x1, Pallas kernels, per_device(): pl.pallas_call(functools.partial(kernel, nz, ny), out_shape=jax.ShapeDtyp...  80.4 us
    unnamed x1, local copies, waits for them, and re-layouts  1.89 us

profile of v2, /device:TPU:1, one launch (start us, length us, event | category | flops | bytes accessed | tf_op | source)
XLA Modules:
  0.0 83.0 jit_solution(13666284963938512447)
XLA Ops:
  0.7 80.4 %correlate.1 = f32[128,1024]{1,0:T(8,128)} custom-call(s32[1,64]{1,0:T(1,128)} %bitcast.9, s32[1,1024]{1,0:T(1,128)} %bitcast.7, s32[1,1024]{1,0:T(1,128)} %bitcast.8, s32[1,1]{1,0:T(1,128)} %bitcast.5.cnt_ref, bf16[256,2,2048]{2,1,0:T(2,128)(2,1)} %bitcast.6, f32[2,33,2048]{2,1,0:T(8,128)} %constant.4.clone.coarse_ref, f32[2,16,2048]{2,1,0:T(8,128)} %constant.5.clone.fine_ref), custom_call_target="tpu_custom_call" | custom-call | tf_op jit(solution)/shard_map/correlate/pallas_call | solution.py:388
  81.1 1.9 %copy.10 = f32[128,1024]{1,0:T(8,128)} copy(f32[128,1024]{1,0:T(8,128)} %correlate.1) | data formatting | bytes 1048576

commit v3 on v2

--- a/solution.py
+++ b/solution.py
@@ -20,7 +20,8 @@
 PAIRS = 2
 PRE = 4
 SKIP = frozenset()
-PACE = (1, 2, 2)
+PACE = (1, 1, 0, 1, 0, 0, 0)
+AHEAD = 2
 
 
 def trig_parts(lags, freq, segs):
@@ -158,24 +159,32 @@
             x2_send.at[r, d - 1], x2_recv.at[r, d - 1], chan=x_peer(d),
         )
 
-    lax.fori_loop(0, chunks, whiten, 0)
-    pl.semaphore_wait(barrier, met)
-    for r in range(rounds):
+    for r in range(rounds):
+        lax.fori_loop(r * NX, (r + 1) * NX, whiten, 0)
+        if r == 0:
+            pl.semaphore_wait(barrier, met)
         for d in range(1, NX):
             x1(r, d).start()
 
-    def send_halo(f, carry):
-        halo_left(f).start()
-        halo_right(f).start()
-        return carry
-
-    paces = [min(sum(PACE[:i]), chunks) for i in range(len(PACE) + 1)] + [chunks]
-
-    def send_some(stage):
-        if "halo" not in SKIP:
-            lax.fori_loop(paces[stage], paces[stage + 1], send_halo, 0)
-
-    send_some(0)
+    fed = [0]
+
+    def feed(count):
+        for _ in range(count):
+            f = fed[0]
+            if f == chunks:
+                return
+            if f >= AHEAD:
+                sent_halo(f - AHEAD)
+            halo_left(f).start()
+            halo_right(f).start()
+            fed[0] += 1
+
+    def sent_halo(f):
+        halo_left(f).wait_send()
+        halo_right(f).wait_send()
+
+    paces = list(PACE)
+    feed(paces.pop(0))
 
     def hots():
         at = poff_ref[...] + band
@@ -208,10 +217,6 @@
         for t in range(tiles):
             rec[t, f] = dot(rows[f], hot_r[t]).astype(jnp.bfloat16)
 
-    def gather_step(f, carry):
-        gather(f)
-        return carry
-
     def wait_halo(f):
         halo_left(f).wait_recv()
         halo_right(f).wait_recv()
@@ -228,7 +233,7 @@
         slab[r] = total
         for d in range(1, nz):
             z1(r, d).start()
-    send_some(1)
+        feed(paces.pop(0))
     for r in range(rounds):
         for d in range(1, nz):
             z1(r, d).wait_recv()
@@ -238,14 +243,16 @@
         srcs[r * NX + mx, mz] = total
         for d in range(1, nz):
             z2(r, d).start()
-    send_some(2)
+        feed(paces.pop(0))
     for r in range(rounds):
         for d in range(1, nz):
             z2(r, d).wait_recv()
         for d in range(1, NX):
             x2(r, d).start()
-    send_some(3)
-    lax.fori_loop(0, pre, gather_step, 0)
+        feed(paces.pop(0))
+    for f in range(pre):
+        gather(f)
+        feed(1)
 
     def cross(f, t, early):
         got = rec[t, f].astype(jnp.float32) if early else dot(rows[f], hot_r[t])
@@ -286,7 +293,10 @@
             else:
                 low = max(low, pre // PAIRS)
             if low < high:
-                lax.fori_loop(low, high, pair_step(early), 0)
+                for i in range(low, high):
+                    pair_step(early)(i, 0)
+                    feed(1)
+    feed(chunks)
     if (rounds - 1) * NX // PAIRS >= pairs - 1:
         wait_sources(rounds - 1)
     for k in range(PAIRS):
@@ -349,13 +359,8 @@
         low = (rest - mid.astype(jnp.float32)).astype(jnp.bfloat16)
         out_ref[:, t * TILE:(t + 1) * TILE] = dot(order, high) + (dot(order, mid) + dot(order, low))
 
-    def halo_sent(f, carry):
-        halo_left(f).wait_send()
-        halo_right(f).wait_send()
-        return carry
-
-    if "halo" not in SKIP:
-        lax.fori_loop(0, chunks, halo_sent, 0)
+    for f in range(max(0, chunks - AHEAD), chunks):
+        sent_halo(f)
     for r in range(rounds):
         for d in range(1, NX):
             x1(r, d).wait_send()

time: 83.2 us -> 75.4 us (0.906)
  Pallas kernels: 80.4 us -> 72.7 us
    pallas_call x1, Pallas kernels: 80.4 us -> 72.7 us  [per_device(): pl.pallas_call(functools.partial(kernel, nz, ny), out_shape=jax.ShapeDtyp...]
where the time goes in v3:
time: 75.4 us; the launch traced here: 75.2 us
  Pallas kernels  72.7 us (96%)
  local copies, waits for them, and re-layouts  1.89 us (3%)
    pallas_call x1, Pallas kernels, per_device(): pl.pallas_call(functools.partial(kernel, nz, ny), out_shape=jax.ShapeDtyp...  72.7 us
    unnamed x1, local copies, waits for them, and re-layouts  1.89 us

profile of v3, /device:TPU:1, one launch (start us, length us, event | category | flops | bytes accessed | tf_op | source)
XLA Modules:
  0.0 75.2 jit_solution(7918599421104030658)
XLA Ops:
  0.7 72.7 %correlate.1 = f32[128,1024]{1,0:T(8,128)} custom-call(s32[1,64]{1,0:T(1,128)} %bitcast.9, s32[1,1024]{1,0:T(1,128)} %bitcast.7, s32[1,1024]{1,0:T(1,128)} %bitcast.8, s32[1,1]{1,0:T(1,128)} %bitcast.5.cnt_ref, bf16[256,2,2048]{2,1,0:T(2,128)(2,1)} %bitcast.6, f32[2,33,2048]{2,1,0:T(8,128)} %constant.4.clone.coarse_ref, f32[2,16,2048]{2,1,0:T(8,128)} %constant.5.clone.fine_ref), custom_call_target="tpu_custom_call" | custom-call | tf_op jit(solution)/shard_map/correlate/pallas_call | solution.py:393
  73.4 1.9 %copy.10 = f32[128,1024]{1,0:T(8,128)} copy(f32[128,1024]{1,0:T(8,128)} %correlate.1) | data formatting | bytes 1048576

commit v4 on v3

--- a/solution.py
+++ b/solution.py
@@ -19,7 +19,6 @@
 FINE = 16
 PAIRS = 2
 PRE = 4
-SKIP = frozenset()
 PACE = (1, 1, 0, 1, 0, 0, 0)
 AHEAD = 2
 
@@ -43,9 +42,9 @@
 def kernel(
     nz, ny, ids_ref, psrc_ref, poff_ref, cnt_ref, raw_hbm, coarse_ref, fine_ref, out_ref,
     raw, tab, rows, pick, slab_in, slab, part_in, srcs, hot_r, hot_s, rec, acc,
-    core_out, core_in, y_out, y_in, y_own,
+    core_out, core_in, relay_out, relay_in, y_out, y_in, y_own,
     raw_sem, halo_send, halo_recv, x1_send, x1_recv, z1_send, z1_recv,
-    z2_send, z2_recv, x2_send, x2_recv, core_send, core_recv, y_send, y_recv,
+    z2_send, z2_recv, x2_send, x2_recv, core_send, core_recv, relay_send, relay_recv, y_send, y_recv,
 ):
     chans = raw.shape[0]
     chunks = rows.shape[0]
@@ -305,10 +304,19 @@
     def to_core(t):
         return remote(core_out.at[t], core_in.at[t], core_send.at[t], core_recv.at[t], seg=other)
 
-    def to_y(t, d):
-        return remote(
-            y_out.at[t, d - 1], y_in.at[t, d - 1],
-            y_send.at[t, d - 1], y_recv.at[t, d - 1], seg=y_peer(d),
+    up, down, far = y_peer(1), y_peer(ny - 1), (my + 2) % ny
+    part = out_rows // 2
+
+    def to_relay(t, side):
+        return remote(
+            relay_out.at[t, side], relay_in.at[t, side],
+            relay_send.at[t, side], relay_recv.at[t, side], seg=(up, down)[side],
+        )
+
+    def to_y(t, side):
+        return remote(
+            y_out.at[t, side], y_in.at[t, side],
+            y_send.at[t, side], y_recv.at[t, side], seg=(up, down)[side],
         )
 
     def lag_block(t, j, parity):
@@ -321,8 +329,6 @@
 
     def finish_tile(t):
         acc[t, 0], acc[t, 1] = pair_sum(pairs - 1, t, False)
-        if "rs" in SKIP:
-            return
         for j in range(ny):
             core_out[t, j] = lag_block(t, j, 1 - mc).astype(jnp.bfloat16)
         to_core(t).start()
@@ -331,16 +337,28 @@
         to_core(t).wait_recv()
         for j in range(ny):
             y_own[t, j] = lag_block(t, j, mc) + core_in[t, j].astype(jnp.float32)
-        for d in range(1, ny):
-            y_out[t, d - 1] = y_own[t, (my + d) % ny].astype(jnp.bfloat16)
-            to_y(t, d).start()
-
-    for t in range(tiles):
-        finish_tile(t)
-        if t and "rs" not in SKIP:
+        for side in range(2):
+            relay_out[t, side] = y_own[t, far, side * part:(side + 1) * part].astype(jnp.bfloat16)
+            to_relay(t, side).start()
+
+    def merge(t):
+        for side, j in enumerate(((my + 1) % ny, (my + ny - 1) % ny)):
+            to_relay(t, side).wait_recv()
+            rest = (1 - side) * part
+            y_out[t, side, side * part:(side + 1) * part] = (
+                y_own[t, j, side * part:(side + 1) * part]
+                + relay_in[t, side].astype(jnp.float32)
+            ).astype(jnp.bfloat16)
+            y_out[t, side, rest:rest + part] = y_own[t, j, rest:rest + part].astype(jnp.bfloat16)
+            to_y(t, side).start()
+
+    for t in range(tiles + 2):
+        if t < tiles:
+            finish_tile(t)
+        if 1 <= t <= tiles:
             pass_on(t - 1)
-    if "rs" not in SKIP:
-        pass_on(tiles - 1)
+        if t >= 2:
+            merge(t - 2)
 
     place = lax.broadcasted_iota(jnp.int32, (out_rows, out_rows), 0)
     place = jnp.where(my >= ny // 2, place, out_rows - 1 - place)
@@ -349,10 +367,9 @@
     ).astype(jnp.bfloat16)
     for t in range(tiles):
         val = y_own[t, my]
-        if "rs" not in SKIP:
-            for d in range(1, ny):
-                to_y(t, d).wait_recv()
-                val = val + y_in[t, d - 1].astype(jnp.float32)
+        for side in range(2):
+            to_y(t, side).wait_recv()
+            val = val + y_in[t, side].astype(jnp.float32)
         high = val.astype(jnp.bfloat16)
         rest = val - high.astype(jnp.float32)
         mid = rest.astype(jnp.bfloat16)
@@ -368,11 +385,11 @@
         for d in range(1, nz):
             z1(r, d).wait_send()
             z2(r, d).wait_send()
-    if "rs" not in SKIP:
-        for t in range(tiles):
-            to_core(t).wait_send()
-            for d in range(1, ny):
-                to_y(t, d).wait_send()
+    for t in range(tiles):
+        to_core(t).wait_send()
+        for side in range(2):
+            to_relay(t, side).wait_send()
+            to_y(t, side).wait_send()
 
 
 def solution(mesh):
@@ -410,8 +427,10 @@
                 pltpu.VMEM((tiles, 2, taus, TILE), f32),
                 pltpu.VMEM((tiles, ny, out_rows, TILE), bf16),
                 pltpu.VMEM((tiles, ny, out_rows, TILE), bf16),
-                pltpu.VMEM((tiles, ny - 1, out_rows, TILE), bf16),
-                pltpu.VMEM((tiles, ny - 1, out_rows, TILE), bf16),
+                pltpu.VMEM((tiles, 2, out_rows // 2, TILE), bf16),
+                pltpu.VMEM((tiles, 2, out_rows // 2, TILE), bf16),
+                pltpu.VMEM((tiles, 2, out_rows, TILE), bf16),
+                pltpu.VMEM((tiles, 2, out_rows, TILE), bf16),
                 pltpu.VMEM((tiles, ny, out_rows, TILE), f32),
                 dma((chunks,)),
                 dma((2, chunks)), dma((2, chunks)),
@@ -420,7 +439,8 @@
                 dma((rounds, nz - 1)), dma((rounds, nz - 1)),
                 dma((rounds, NX - 1)), dma((rounds, NX - 1)),
                 dma((tiles,)), dma((tiles,)),
-                dma((tiles, ny - 1)), dma((tiles, ny - 1)),
+                dma((tiles, 2)), dma((tiles, 2)),
+                dma((tiles, 2)), dma((tiles, 2)),
             ],
             compiler_params=pltpu.CompilerParams(
                 collective_id=0, has_side_effects=True, vmem_limit_bytes=58 << 20

time: 75.4 us -> 73.1 us (0.969)
  Pallas kernels: 72.7 us -> 70.1 us
    pallas_call x1, Pallas kernels: 72.7 us -> 70.1 us  [per_device(): pl.pallas_call(functools.partial(kernel, nz, ny), out_shape=jax.ShapeDtyp...]
where the time goes in v4:
time: 73.1 us; the launch traced here: 72.6 us
  Pallas kernels  70.1 us (96%)
  local copies, waits for them, and re-layouts  1.89 us (3%)
    pallas_call x1, Pallas kernels, per_device(): pl.pallas_call(functools.partial(kernel, nz, ny), out_shape=jax.ShapeDtyp...  70.1 us
    unnamed x1, local copies, waits for them, and re-layouts  1.89 us

profile of v4, /device:TPU:1, one launch (start us, length us, event | category | flops | bytes accessed | tf_op | source)
XLA Modules:
  0.0 72.6 jit_solution(3559906150468448516)
XLA Ops:
  0.7 70.1 %correlate.1 = f32[128,1024]{1,0:T(8,128)} custom-call(s32[1,64]{1,0:T(1,128)} %bitcast.9, s32[1,1024]{1,0:T(1,128)} %bitcast.7, s32[1,1024]{1,0:T(1,128)} %bitcast.8, s32[1,1]{1,0:T(1,128)} %bitcast.5.cnt_ref, bf16[256,2,2048]{2,1,0:T(2,128)(2,1)} %bitcast.6, f32[2,33,2048]{2,1,0:T(8,128)} %constant.4.clone.coarse_ref, f32[2,16,2048]{2,1,0:T(8,128)} %constant.5.clone.fine_ref), custom_call_target="tpu_custom_call" | custom-call | tf_op jit(solution)/shard_map/correlate/pallas_call | solution.py:410
  70.8 1.9 %copy.10 = f32[128,1024]{1,0:T(8,128)} copy(f32[128,1024]{1,0:T(8,128)} %correlate.1) | data formatting | bytes 1048576

commit v5 on v4

--- a/solution.py
+++ b/solution.py
@@ -18,7 +18,7 @@
 NX = 4
 FINE = 16
 PAIRS = 2
-PRE = 4
+PRE = 2
 PACE = (1, 1, 0, 1, 0, 0, 0)
 AHEAD = 2
 

time: 73.1 us -> 76 us (1.040)
  Pallas kernels: 70.1 us -> 73.3 us
    pallas_call x1, Pallas kernels: 70.1 us -> 73.3 us  [per_device(): pl.pallas_call(functools.partial(kernel, nz, ny), out_shape=jax.ShapeDtyp...]
where the time goes in v5:
time: 76 us; the launch traced here: 75.8 us
  Pallas kernels  73.3 us (96%)
  local copies, waits for them, and re-layouts  1.89 us (2%)
    pallas_call x1, Pallas kernels, per_device(): pl.pallas_call(functools.partial(kernel, nz, ny), out_shape=jax.ShapeDtyp...  73.3 us
    unnamed x1, local copies, waits for them, and re-layouts  1.89 us

profile of v5, /device:TPU:1, one launch (start us, length us, event | category | flops | bytes accessed | tf_op | source)
XLA Modules:
  0.0 75.8 jit_solution(2186759654872450470)
XLA Ops:
  0.7 73.3 %correlate.1 = f32[128,1024]{1,0:T(8,128)} custom-call(s32[1,64]{1,0:T(1,128)} %bitcast.9, s32[1,1024]{1,0:T(1,128)} %bitcast.7, s32[1,1024]{1,0:T(1,128)} %bitcast.8, s32[1,1]{1,0:T(1,128)} %bitcast.5.cnt_ref, bf16[256,2,2048]{2,1,0:T(2,128)(2,1)} %bitcast.6, f32[2,33,2048]{2,1,0:T(8,128)} %constant.4.clone.coarse_ref, f32[2,16,2048]{2,1,0:T(8,128)} %constant.5.clone.fine_ref), custom_call_target="tpu_custom_call" | custom-call | tf_op jit(solution)/shard_map/correlate/pallas_call | solution.py:410
  73.9 1.9 %copy.10 = f32[128,1024]{1,0:T(8,128)} copy(f32[128,1024]{1,0:T(8,128)} %correlate.1) | data formatting | bytes 1048576
